TPU v7x, 32 devices: a whole 2x2x4 slice. The times are simulated.
32 devices in a mesh: group: 2 (over x), expert: 16 (over z, y, core).
Axes of the slice: x: 2, y: 2, z: 4, core: 2. Of those that a mesh axis runs over, the one named last changes fastest.
Arguments:
- tokens: bfloat16 [128, 7168], P(('group', 'expert')), parts along dimension 0, may hold values from -6 to 6
- expert_ids: int32 [128, 2], P(('group', 'expert')), parts along dimension 0, may hold values from 0 to 1, all different within a row; in each aligned block of 4 rows (0 to 3, 4 to 7, ...) at most 4 rows name the same one
- gate_codes: int32 [128, 2], P(('group', 'expert')), parts along dimension 0, may hold values from 1 to 65535
- gate_weight: bfloat16 [16, 7168, 256], P('expert'), may hold values from -0.0625 to 0.0625
- up_weight: bfloat16 [16, 7168, 256], P('expert'), may hold values from -0.0625 to 0.0625
- down_weight: bfloat16 [16, 256, 7168], P('expert'), may hold values from -0.125 to 0.125
- target_basis: bfloat16 [7168, 512], P('expert'), may hold values from -0.0625 to 0.0625
Outputs:
- targets: bfloat16 [128, 512], P(('group', 'expert')), parts along dimension 0
There are 2 independent parts, one for each index of `group`. A program takes and returns all parts, laid end to end along the dimension named above; an argument that names none is the same for every part. Nothing has to cross between parts.
Inputs may be any that keep to these rules, and one draw needn't show every extreme that they name: `expert_ids`: each row names 2 different experts; among the 4 rows of one device no expert is named more than 4 times, a bound that some block reaches.
All inputs are finite; a program needn't handle non-finite values.
Results may differ from a plain program's by a relative error of at most 0.0057.
Values may be sent and summed in bfloat16 or wider, within the bound.
No kernel may reach another device: no remote copies, remote signals or barrier semaphores. Data moves between devices by JAX's collectives and lax.ppermute only.
A program may use at most 128 MiB of HBM per device.

v0:
```python
import jax
import jax.numpy as jnp
from jax import lax
from jax.sharding import PartitionSpec as P

SLICES = 8


def run_expert(received, gate_weight, up_weight, down_weight):
    sources, slots, feature_width = received.shape
    row_block = received.reshape(sources * slots, feature_width)
    gate_act = jnp.dot(row_block, gate_weight[0], preferred_element_type=jnp.float32)
    up_act = jnp.dot(row_block, up_weight[0], preferred_element_type=jnp.float32)
    hidden = (jax.nn.silu(gate_act) * up_act).astype(jnp.bfloat16)
    expert_part = jnp.dot(hidden, down_weight[0], preferred_element_type=jnp.float32).astype(
        jnp.bfloat16
    )
    return expert_part.reshape(sources, slots, feature_width)


def shards(tokens, expert_ids, gate_codes, gate_weight, up_weight, down_weight, target_basis):
    token_count, feature_width = tokens.shape
    pick_count = expert_ids.shape[1]
    owner_count = lax.axis_size("expert")
    expert_count = owner_count // SLICES
    capacity = min(token_count, max(2, 5 * token_count * pick_count // (4 * expert_count)))
    rank_width = target_basis.shape[1]
    flat_ids = expert_ids.reshape(-1)
    onehot = (flat_ids[:, None] == jnp.arange(expert_count, dtype=jnp.int32)[None, :]).astype(
        jnp.int32
    )
    before = jnp.cumsum(onehot, axis=0) - onehot
    slot_rank = jnp.sum(before * onehot, axis=1)
    slot_index = flat_ids * capacity + slot_rank
    row_token = jnp.arange(token_count * pick_count, dtype=jnp.int32) // pick_count
    slot_table = (
        jnp.full((expert_count * capacity,), token_count, jnp.int32).at[slot_index].set(row_token)
    )
    padded = jnp.concatenate([tokens, jnp.zeros((1, feature_width), tokens.dtype)], axis=0)
    per_expert_rows = padded[slot_table].reshape(expert_count, 1, capacity, feature_width)
    outgoing = jnp.broadcast_to(per_expert_rows, (expert_count, SLICES, capacity, feature_width))
    outgoing = outgoing.reshape(owner_count, capacity, feature_width)
    full_basis = lax.all_gather(target_basis, "expert", axis=0, tiled=True)
    expert_part = run_expert(
        lax.all_to_all(outgoing, "expert", split_axis=0, concat_axis=0, tiled=True),
        gate_weight,
        up_weight,
        down_weight,
    )
    result = jnp.einsum("skd,dr->skr", expert_part, full_basis, preferred_element_type=jnp.float32)
    returned = lax.all_to_all(result, "expert", split_axis=0, concat_axis=0, tiled=True)
    summed = jnp.sum(returned.reshape(expert_count, SLICES, capacity, rank_width), axis=1)
    projected = summed.reshape(expert_count * capacity, rank_width)[slot_index]
    codes_float = gate_codes.astype(jnp.float32)
    weights = 2.5 * codes_float / jnp.sum(codes_float, axis=1, keepdims=True)
    projected = projected.reshape(token_count, pick_count, rank_width)
    return jnp.sum(weights[:, :, None] * projected, axis=1).astype(jnp.bfloat16)


def solution(mesh):
    in_specs = (
        P(("group", "expert"), None),
        P(("group", "expert"), None),
        P(("group", "expert"), None),
        P("expert", None, None),
        P("expert", None, None),
        P("expert", None, None),
        P("expert", None),
    )
    out_specs = P(("group", "expert"), None)
    return jax.shard_map(shards, mesh=mesh, in_specs=in_specs, out_specs=out_specs, check_vma=False)
```

profile of v0, /device:TPU:0, one launch (start us, length us, event | category | flops | bytes accessed | tf_op | source)
XLA Modules:
  0.0 121.8 jit_solution(8186890199680378276)
XLA Ops:
  6.5 0.0 copy-start
  6.5 0.0 all-gather.2.cloned.1.call-start
  6.5 0.7 all-gather.2.cloned.1.call-update
  7.3 0.8 copy.25
  8.0 0.1 eq.15
  8.1 0.7 broadcast_multiply_fusion
  8.8 0.1 copy.24
  8.9 0.1 mul.37
  9.0 0.2 reduce_window_sum.11
  9.2 0.8 concatenate.3
  10.1 0.6 scatter_custom_fusion
  10.7 0.6 gather_fusion
  11.3 0.1 broadcast_in_dim.7
  11.4 1.2 broadcast_in_dim.8
  12.5 7.4 %all-to-all-start = ((bf16[16,4,7168]{2,1,0:T(4,128)(2,1)}), bf16[16,4,7168]{2,1,0:T(4,128)(2,1)S(1)}, u32[]{:S(2)}, u32[]{:S(2)}) async-start(bf16[16,4,7168]{2,1,0:T(4,128)(2,1)} %bitcast.2), calls=%async_computation | async-start | bytes 1835008 | tf_op jit(solution)/shard_map/all_to_all | solution.py:45
  19.9 0.0 copy-done
  20.0 35.1 %all-to-all-done = bf16[16,4,7168]{2,1,0:T(4,128)(2,1)S(1)} async-done(((bf16[16,4,7168]{2,1,0:T(4,128)(2,1)}), bf16[16,4,7168]{2,1,0:T(4,128)(2,1)S(1)}, u32[]{:S(2)}, u32[]{:S(2)}) %all-to-all-start) | async-done | bytes 917536 | tf_op jit(solution)/shard_map/all_to_all | solution.py:45
  55.1 0.2 reshape.53
  55.3 2.8 %fusion.5 = f32[64,256]{1,0:T(8,128)S(1)} fusion(bf16[64,7168]{1,0:T(8,128)(2,1)S(1)} %reshape.53, bf16[1,7168,256]{2,1,0:T(8,128)(2,1)} %param.10), kind=kOutput, calls=%fused_computation.9 | convolution fusion | flops 234881024 | bytes 4653056 | tf_op jit(solution)/shard_map/dot_general | solution.py:12
  58.0 5.5 %convolution_convert_fusion = bf16[64,7168]{1,0:T(8,128)(2,1)S(1)} fusion(bf16[1,256,7168]{2,1,0:T(8,128)(2,1)} %param.12, bf16[64,7168]{1,0:T(8,128)(2,1)S(1)} %reshape.53, bf16[1,7168,256]{2,1,0:T(8,128)(2,1)} %param.11, f32[64,256]{1,0:T(8,128)S(1)} %fusion.5), kind=kOutput, calls=%fused_computation.3 | convolution fusion | flops 470319104 | bytes 9240576 | tf_op jit(solution)/shard_map/dot_general | solution.py:15
  63.5 0.3 reshape.54
  63.8 33.4 %all-gather.2.cloned.1.call-done = bf16[7168,512]{1,0:T(8,128)(2,1)} async-done(((bf16[448,512]{1,0:T(8,128)(2,1)}), bf16[7168,512]{1,0:T(8,128)(2,1)}) %all-gather.2.cloned.1.call-update) | async-done | bytes 7340048 | tf_op jit(solution)/shard_map/all_gather | solution.py:43
  97.3 4.2 %fusion = f32[16,4,512]{2,0,1:T(8,128)S(1)} fusion(bf16[7168,512]{1,0:T(8,128)(2,1)} %all-gather.2.cloned.1.call-done, bf16[16,4,7168]{2,1,0:T(4,128)(2,1)S(1)} %reshape.54), kind=kOutput, calls=%fused_computation.4 | convolution fusion | flops 469762048 | bytes 8388608 | tf_op jit(solution)/shard_map/skd,dr->skr/dot_general | solution.py:50
  101.5 0.7 copy.27
  102.2 3.5 %all-to-all-start.1 = ((f32[16,4,512]{2,1,0:T(4,128)}), f32[16,4,512]{2,1,0:T(4,128)S(1)}, u32[]{:S(2)}, u32[]{:S(2)}) async-start(f32[16,4,512]{2,1,0:T(4,128)} %copy.27), calls=%async_computation.1 | async-start | bytes 262144 | tf_op jit(solution)/shard_map/all_to_all | solution.py:51
  105.8 0.1 copy.23
  105.9 7.8 %all-to-all-done.1 = f32[16,4,512]{2,1,0:T(4,128)S(1)} async-done(((f32[16,4,512]{2,1,0:T(4,128)}), f32[16,4,512]{2,1,0:T(4,128)S(1)}, u32[]{:S(2)}, u32[]{:S(2)}) %all-to-all-start.1) | async-done | bytes 131104 | tf_op jit(solution)/shard_map/all_to_all | solution.py:51
  113.7 0.6 gather_fusion.1
  114.2 0.7 multiply_reduce_fusion
  (12 shorter events, 0.1 us)
Async XLA Ops:
  6.5 13.4 %copy-start = (s32[4,2]{0,1:T(2,128)S(1)}, s32[4,2]{0,1:T(2,128)}, u32[]{:S(2)}) copy-start(s32[4,2]{0,1:T(2,128)} %param.9) | copy-start | bytes 100
  6.5 90.7 %all-gather.2.cloned.1.call-start = ((), (), s32[]{:S(2)}) async-start(), calls=%async_computation.2 | async-start | bytes 7798784 | tf_op jit(solution)/shard_map/all_gather | solution.py:43
  12.5 42.5 %all-to-all-start = ((bf16[16,4,7168]{2,1,0:T(4,128)(2,1)}), bf16[16,4,7168]{2,1,0:T(4,128)(2,1)S(1)}, u32[]{:S(2)}, u32[]{:S(2)}) async-start(bf16[16,4,7168]{2,1,0:T(4,128)(2,1)} %bitcast.2), calls=%async_computation | async-start | bytes 1835008 | tf_op jit(solution)/shard_map/all_to_all | solution.py:45
  102.2 11.4 %all-to-all-start.1 = ((f32[16,4,512]{2,1,0:T(4,128)}), f32[16,4,512]{2,1,0:T(4,128)S(1)}, u32[]{:S(2)}, u32[]{:S(2)}) async-start(f32[16,4,512]{2,1,0:T(4,128)} %copy.27), calls=%async_computation.1 | async-start | bytes 262144 | tf_op jit(solution)/shard_map/all_to_all | solution.py:51
Sparse Core Ops, SparseCore 0:
  9.6 87.5 all-gather.1
where the time goes:
time: 122 us
  waiting for transfers between devices  77 us (63%)
  between operations  13.5 us (11%)
  matrix products  12.4 us (10%)
  starting transfers between devices  10.9 us (9%)
  local copies, waits for them, and re-layouts  6.25 us (5%)
  other arithmetic  1.66 us (1%)
    all_to_all x1, waiting for transfers between devices, shards(): lax.all_to_all(outgoing, 'expert', split_axis=0, concat_axis=0, tiled=True)  35.1 us
    all_gather x1, waiting for transfers between devices, shards(): full_basis = lax.all_gather(target_basis, 'expert', axis=0, tiled=True)  33.4 us
    all_to_all x1, waiting for transfers between devices, shards(): lax.all_to_all(result, 'expert', split_axis=0, concat_axis=0, tiled=True)  7.76 us
    all_to_all x1, starting transfers between devices, shards(): lax.all_to_all(outgoing, 'expert', split_axis=0, concat_axis=0, tiled=True)  7.41 us
    dot_general x1, matrix products, run_expert(): jnp.dot(hidden, down_weight[0], preferred_element_type=jnp.float32)  5.45 us
    dot_general x1, matrix products, shards(): jnp.einsum('skd,dr->skr', expert_part, full_basis, preferred_element_type...  4.23 us
    all_to_all x1, starting transfers between devices, shards(): lax.all_to_all(result, 'expert', split_axis=0, concat_axis=0, tiled=True)  3.51 us
    dot_general x1, matrix products, run_expert(): jnp.dot(row_block, gate_weight[0], preferred_element_type=jnp.float32)  2.76 us
  transfers between devices with their start and end apart: 3, of which 3 were waited for; matrix products, arithmetic and copies ran while one was open for 12% of the time, Pallas kernels for 0%

commit v1 on v0

--- a/solution.py
+++ b/solution.py
@@ -40,7 +40,14 @@
     per_expert_rows = padded[slot_table].reshape(expert_count, 1, capacity, feature_width)
     outgoing = jnp.broadcast_to(per_expert_rows, (expert_count, SLICES, capacity, feature_width))
     outgoing = outgoing.reshape(owner_count, capacity, feature_width)
-    full_basis = lax.all_gather(target_basis, "expert", axis=0, tiled=True)
+    ring = [target_basis]
+    for hop in range(15):
+        ring.append(lax.ppermute(ring[-1], "expert", [(dev, (dev + 1) % 16) for dev in range(16)]))
+    full_basis = jnp.roll(
+        jnp.concatenate(ring[::-1], axis=0),
+        (lax.axis_index("expert") + 1) * ring[0].shape[0],
+        axis=0,
+    )
     expert_part = run_expert(
         lax.all_to_all(outgoing, "expert", split_axis=0, concat_axis=0, tiled=True),
         gate_weight,

time: 122 us -> 212 us (1.74)
  waiting for transfers between devices: 77 us -> 160 us
  local copies, waits for them, and re-layouts: 6.25 us -> 28.6 us
  between operations: 13.5 us -> 0.53 us
    ppermute x0 -> x15, waiting for transfers between devices: none -> 152 us  [shards(): lax.ppermute(ring[-1], 'expert', [(dev, (dev + 1) % 16) for dev in range(...]
    all_to_all x1, waiting for transfers between devices: 35.1 us -> 0.01 us  [shards(): lax.all_to_all(outgoing, 'expert', split_axis=0, concat_axis=0, tiled=True)]
    all_gather x1 -> x0, waiting for transfers between devices: 33.4 us -> none  [shards(): full_basis = lax.all_gather(target_basis, 'expert', axis=0, tiled=True)]
    unnamed x3 -> x80, local copies, waits for them, and re-layouts: 0.77 us -> 23.1 us
    dot_general x1, matrix products: 4.23 us -> 2.06 us  [shards(): jnp.einsum('skd,dr->skr', expert_part, full_basis, preferred_element_type...]
  transfers between devices with their start and end apart: 3 -> 17, of which waited for: 3 -> 16; matrix products, arithmetic and copies ran while one was open for 12% -> 7% of each run, Pallas kernels for 0% -> 0%
where the time goes in v1:
time: 212 us; the launch traced here: 211 us
  waiting for transfers between devices  160 us (75%)
  local copies, waits for them, and re-layouts  28.6 us (13%)
  matrix products  10.3 us (5%)
  starting transfers between devices  9.85 us (5%)
  other arithmetic  2.33 us (1%)
    ppermute x15, waiting for transfers between devices, shards(): lax.ppermute(ring[-1], 'expert', [(dev, (dev + 1) % 16) for dev in range(...  152 us
    unnamed x80, local copies, waits for them, and re-layouts  23.1 us
    all_to_all x1, waiting for transfers between devices, shards(): lax.all_to_all(result, 'expert', split_axis=0, concat_axis=0, tiled=True)  7.75 us
    all_to_all x1, starting transfers between devices, shards(): lax.all_to_all(outgoing, 'expert', split_axis=0, concat_axis=0, tiled=True)  5.81 us
    dot_general x1, matrix products, run_expert(): jnp.dot(hidden, down_weight[0], preferred_element_type=jnp.float32)  5.45 us
  transfers between devices with their start and end apart: 17, of which 16 were waited for; matrix products, arithmetic and copies ran while one was open for 7% of the time, Pallas kernels for 0%

profile of v1, /device:TPU:0, one launch (start us, length us, event | category | flops | bytes accessed | tf_op | source)
XLA Modules:
  0.0 211.3 jit_solution(14295122072014855219)
XLA Ops:
  0.0 0.5 collective-permute-start
  0.5 11.4 %collective-permute-done = bf16[448,512]{1,0:T(8,128)(2,1)S(1)} collective-permute-done((bf16[448,512]{1,0:T(8,128)(2,1)}, bf16[448,512]{1,0:T(8,128)(2,1)S(1)}, u32[]{:S(2)}, u32[]{:S(2)}) %collective-permute-start) | collective-permute-done | bytes 458784 | tf_op jit(solution)/shard_map/ppermute | solution.py:45
  11.8 10.6 %collective-permute-done.1 = bf16[448,512]{1,0:T(8,128)(2,1)S(1)} collective-permute-done((bf16[448,512]{1,0:T(8,128)(2,1)S(1)}, bf16[448,512]{1,0:T(8,128)(2,1)S(1)}, u32[]{:S(2)}, u32[]{:S(2)}) %collective-permute-start.1) | collective-permute-done | bytes 458784 | tf_op jit(solution)/shard_map/ppermute | solution.py:45
  22.4 0.8 copy-done.1
  23.3 10.6 %collective-permute-done.2 = bf16[448,512]{1,0:T(8,128)(2,1)S(1)} collective-permute-done((bf16[448,512]{1,0:T(8,128)(2,1)S(1)}, bf16[448,512]{1,0:T(8,128)(2,1)S(1)}, u32[]{:S(2)}, u32[]{:S(2)}) %collective-permute-start.2) | collective-permute-done | bytes 458784 | tf_op jit(solution)/shard_map/ppermute | solution.py:45
  33.9 0.8 copy-done.3
  34.6 10.6 %collective-permute-done.3 = bf16[448,512]{1,0:T(8,128)(2,1)S(1)} collective-permute-done((bf16[448,512]{1,0:T(8,128)(2,1)S(1)}, bf16[448,512]{1,0:T(8,128)(2,1)S(1)}, u32[]{:S(2)}, u32[]{:S(2)}) %collective-permute-start.3) | collective-permute-done | bytes 458784 | tf_op jit(solution)/shard_map/ppermute | solution.py:45
  45.2 0.8 copy-done.5
  46.0 10.6 %collective-permute-done.4 = bf16[448,512]{1,0:T(8,128)(2,1)S(1)} collective-permute-done((bf16[448,512]{1,0:T(8,128)(2,1)S(1)}, bf16[448,512]{1,0:T(8,128)(2,1)S(1)}, u32[]{:S(2)}, u32[]{:S(2)}) %collective-permute-start.4) | collective-permute-done | bytes 458784 | tf_op jit(solution)/shard_map/ppermute | solution.py:45
  56.6 0.8 copy-done.7
  57.4 10.6 %collective-permute-done.5 = bf16[448,512]{1,0:T(8,128)(2,1)S(1)} collective-permute-done((bf16[448,512]{1,0:T(8,128)(2,1)S(1)}, bf16[448,512]{1,0:T(8,128)(2,1)S(1)}, u32[]{:S(2)}, u32[]{:S(2)}) %collective-permute-start.5) | collective-permute-done | bytes 458784 | tf_op jit(solution)/shard_map/ppermute | solution.py:45
  68.0 0.8 copy-done.9
  68.8 10.6 %collective-permute-done.6 = bf16[448,512]{1,0:T(8,128)(2,1)S(1)} collective-permute-done((bf16[448,512]{1,0:T(8,128)(2,1)S(1)}, bf16[448,512]{1,0:T(8,128)(2,1)S(1)}, u32[]{:S(2)}, u32[]{:S(2)}) %collective-permute-start.6) | collective-permute-done | bytes 458784 | tf_op jit(solution)/shard_map/ppermute | solution.py:45
  79.4 0.8 copy.25
  80.1 0.1 eq.18
  80.2 0.7 broadcast_multiply_fusion
  80.9 9.1 %collective-permute-done.7 = bf16[448,512]{1,0:T(8,128)(2,1)S(1)} collective-permute-done((bf16[448,512]{1,0:T(8,128)(2,1)S(1)}, bf16[448,512]{1,0:T(8,128)(2,1)S(1)}, u32[]{:S(2)}, u32[]{:S(2)}) %collective-permute-start.7) | collective-permute-done | bytes 458784 | tf_op jit(solution)/shard_map/ppermute | solution.py:45
  90.0 0.1 copy.24
  90.1 0.1 mul.40
  90.2 0.2 reduce_window_sum.11
  90.4 0.8 concatenate.9
  91.2 0.6 scatter_custom_fusion
  91.9 8.7 %collective-permute-done.8 = bf16[448,512]{1,0:T(8,128)(2,1)S(1)} collective-permute-done((bf16[448,512]{1,0:T(8,128)(2,1)S(1)}, bf16[448,512]{1,0:T(8,128)(2,1)S(1)}, u32[]{:S(2)}, u32[]{:S(2)}) %collective-permute-start.8) | collective-permute-done | bytes 458784 | tf_op jit(solution)/shard_map/ppermute | solution.py:45
  100.6 0.6 gather_fusion
  101.2 0.1 broadcast_in_dim.7
  101.3 1.2 broadcast_in_dim.8
  102.5 5.8 %all-to-all-start = ((bf16[16,4,7168]{2,1,0:T(4,128)(2,1)}), bf16[16,4,7168]{2,1,0:T(4,128)(2,1)S(1)}, u32[]{:S(2)}, u32[]{:S(2)}) async-start(bf16[16,4,7168]{2,1,0:T(4,128)(2,1)} %bitcast.2), calls=%async_computation | async-start | bytes 1835008 | tf_op jit(solution)/shard_map/all_to_all | solution.py:52
  108.3 2.9 %collective-permute-done.9 = bf16[448,512]{1,0:T(8,128)(2,1)S(1)} collective-permute-done((bf16[448,512]{1,0:T(8,128)(2,1)S(1)}, bf16[448,512]{1,0:T(8,128)(2,1)S(1)}, u32[]{:S(2)}, u32[]{:S(2)}) %collective-permute-start.9) | collective-permute-done | bytes 458784 | tf_op jit(solution)/shard_map/ppermute | solution.py:45
  111.2 22.8 %collective-permute-done.10 = bf16[448,512]{1,0:T(8,128)(2,1)S(1)} collective-permute-done((bf16[448,512]{1,0:T(8,128)(2,1)S(1)}, bf16[448,512]{1,0:T(8,128)(2,1)S(1)}, u32[]{:S(2)}, u32[]{:S(2)}) %collective-permute-start.10) | collective-permute-done | bytes 458784 | tf_op jit(solution)/shard_map/ppermute | solution.py:45
  134.0 10.6 %collective-permute-done.11 = bf16[448,512]{1,0:T(8,128)(2,1)S(1)} collective-permute-done((bf16[448,512]{1,0:T(8,128)(2,1)S(1)}, bf16[448,512]{1,0:T(8,128)(2,1)S(1)}, u32[]{:S(2)}, u32[]{:S(2)}) %collective-permute-start.11) | collective-permute-done | bytes 458784 | tf_op jit(solution)/shard_map/ppermute | solution.py:45
  144.6 10.7 %collective-permute-done.12 = bf16[448,512]{1,0:T(8,128)(2,1)} collective-permute-done((bf16[448,512]{1,0:T(8,128)(2,1)S(1)}, bf16[448,512]{1,0:T(8,128)(2,1)}, u32[]{:S(2)}, u32[]{:S(2)}) %collective-permute-start.12) | collective-permute-done | bytes 458784 | tf_op jit(solution)/shard_map/ppermute | solution.py:45
  155.3 0.7 convert_reduce_fusion
  156.0 0.2 reshape.53
  156.2 0.0 copy-start
  156.2 2.8 %fusion.6 = f32[64,256]{1,0:T(8,128)S(1)} fusion(bf16[64,7168]{1,0:T(8,128)(2,1)S(1)} %reshape.53, bf16[1,7168,256]{2,1,0:T(8,128)(2,1)} %param.10), kind=kOutput, calls=%fused_computation.10 | convolution fusion | flops 234881024 | bytes 4653056 | tf_op jit(solution)/shard_map/dot_general | solution.py:12
  159.1 7.2 %collective-permute-done.13 = bf16[448,512]{1,0:T(8,128)(2,1)} collective-permute-done((bf16[448,512]{1,0:T(8,128)(2,1)}, bf16[448,512]{1,0:T(8,128)(2,1)}, u32[]{:S(2)}, u32[]{:S(2)}) %collective-permute-start.13) | collective-permute-done | bytes 458784 | tf_op jit(solution)/shard_map/ppermute | solution.py:45
  166.2 5.5 %convolution_convert_fusion = bf16[64,7168]{1,0:T(8,128)(2,1)S(1)} fusion(bf16[1,256,7168]{2,1,0:T(8,128)(2,1)} %param.12, bf16[64,7168]{1,0:T(8,128)(2,1)S(1)} %reshape.53, bf16[1,7168,256]{2,1,0:T(8,128)(2,1)} %param.11, f32[64,256]{1,0:T(8,128)S(1)} %fusion.6), kind=kOutput, calls=%fused_computation.3 | convolution fusion | flops 470319104 | bytes 9240576 | tf_op jit(solution)/shard_map/dot_general | solution.py:15
  171.7 0.3 reshape.54
  172.1 5.0 %collective-permute-done.14 = bf16[448,512]{1,0:T(8,128)(2,1)} collective-permute-done((bf16[448,512]{1,0:T(8,128)(2,1)}, bf16[448,512]{1,0:T(8,128)(2,1)}, u32[]{:S(2)}, u32[]{:S(2)}) %collective-permute-start.14) | collective-permute-done | bytes 458784 | tf_op jit(solution)/shard_map/ppermute | solution.py:45
  177.1 1.0 constant_dynamic-update-slice_fusion.31
  178.2 1.1 constant_dynamic-update-slice_fusion.30
  179.2 1.1 constant_dynamic-update-slice_fusion.29
  180.3 1.1 constant_dynamic-update-slice_fusion.28
  181.4 1.1 constant_dynamic-update-slice_fusion.27
  182.4 1.1 constant_dynamic-update-slice_fusion.26
  183.5 1.1 constant_dynamic-update-slice_fusion.25
  184.5 1.1 constant_dynamic-update-slice_fusion.24
  185.6 1.1 constant_dynamic-update-slice_fusion.23
  186.6 1.1 constant_dynamic-update-slice_fusion.22
  187.7 0.0 copy-start.23
  187.7 1.1 constant_dynamic-update-slice_fusion.21
  188.7 1.1 constant_dynamic-update-slice_fusion.20
  189.8 1.1 constant_dynamic-update-slice_fusion.19
  190.9 1.1 constant_dynamic-update-slice_fusion.18
  192.0 1.1 constant_dynamic-update-slice_fusion.15
  193.0 1.1 constant_dynamic-update-slice_fusion.14
  194.1 1.1 constant_dynamic-update-slice_fusion.13
  195.8 2.1 fusion
  197.9 0.7 copy.27
  198.6 3.5 %all-to-all-start.1 = ((f32[16,4,512]{2,1,0:T(4,128)}), f32[16,4,512]{2,1,0:T(4,128)S(1)}, u32[]{:S(2)}, u32[]{:S(2)}) async-start(f32[16,4,512]{2,1,0:T(4,128)} %copy.27), calls=%async_computation.1 | async-start | bytes 262144 | tf_op jit(solution)/shard_map/all_to_all | solution.py:58
  202.1 0.1 copy.23
  202.2 7.7 %all-to-all-done.1 = f32[16,4,512]{2,1,0:T(4,128)S(1)} async-done(((f32[16,4,512]{2,1,0:T(4,128)}), f32[16,4,512]{2,1,0:T(4,128)S(1)}, u32[]{:S(2)}, u32[]{:S(2)}) %all-to-all-start.1) | async-done | bytes 131104 | tf_op jit(solution)/shard_map/all_to_all | solution.py:58
  210.0 0.6 gather_fusion.1
  210.6 0.7 multiply_reduce_fusion
  (82 shorter events, 0.7 us)
Async XLA Ops:
  0.0 11.8 %collective-permute-start = (bf16[448,512]{1,0:T(8,128)(2,1)}, bf16[448,512]{1,0:T(8,128)(2,1)S(1)}, u32[]{:S(2)}, u32[]{:S(2)}) collective-permute-start(bf16[448,512]{1,0:T(8,128)(2,1)} %param.13), channel_id=1, source_target_pairs={{0,1},{1,2},{2,3},{3,4},{4,5},{5,6},{6,7},{7,8},{8,9},{9,10},{10,1... | collective-permute-start | bytes 1376264 | tf_op jit(solution)/shard_map/ppermute | solution.py:45
  11.8 10.6 %collective-permute-start.1 = (bf16[448,512]{1,0:T(8,128)(2,1)S(1)}, bf16[448,512]{1,0:T(8,128)(2,1)S(1)}, u32[]{:S(2)}, u32[]{:S(2)}) collective-permute-start(bf16[448,512]{1,0:T(8,128)(2,1)S(1)} %collective-permute-done), channel_id=1, source_target_pairs={{0,1},{1,2},{2,3},{3,4},{4,5},{5,6},{6,7},{7,8},{8,9},{9,10},{10,1... | collective-permute-start | bytes 1376264 | tf_op jit(solution)/shard_map/ppermute | solution.py:45
  22.4 0.8 copy-start.1
  23.3 10.6 %collective-permute-start.2 = (bf16[448,512]{1,0:T(8,128)(2,1)S(1)}, bf16[448,512]{1,0:T(8,128)(2,1)S(1)}, u32[]{:S(2)}, u32[]{:S(2)}) collective-permute-start(bf16[448,512]{1,0:T(8,128)(2,1)S(1)} %collective-permute-done.1), channel_id=1, source_target_pairs={{0,1},{1,2},{2,3},{3,4},{4,5},{5,6},{6,7},{7,8},{8,9},{9,10},{10,1... | collective-permute-start | bytes 1376264 | tf_op jit(solution)/shard_map/ppermute | solution.py:45
  33.9 0.8 copy-start.3
  34.6 10.6 %collective-permute-start.3 = (bf16[448,512]{1,0:T(8,128)(2,1)S(1)}, bf16[448,512]{1,0:T(8,128)(2,1)S(1)}, u32[]{:S(2)}, u32[]{:S(2)}) collective-permute-start(bf16[448,512]{1,0:T(8,128)(2,1)S(1)} %collective-permute-done.2), channel_id=1, source_target_pairs={{0,1},{1,2},{2,3},{3,4},{4,5},{5,6},{6,7},{7,8},{8,9},{9,10},{10,1... | collective-permute-start | bytes 1376264 | tf_op jit(solution)/shard_map/ppermute | solution.py:45
  45.2 0.8 copy-start.5
  46.0 10.6 %collective-permute-start.4 = (bf16[448,512]{1,0:T(8,128)(2,1)S(1)}, bf16[448,512]{1,0:T(8,128)(2,1)S(1)}, u32[]{:S(2)}, u32[]{:S(2)}) collective-permute-start(bf16[448,512]{1,0:T(8,128)(2,1)S(1)} %collective-permute-done.3), channel_id=1, source_target_pairs={{0,1},{1,2},{2,3},{3,4},{4,5},{5,6},{6,7},{7,8},{8,9},{9,10},{10,1... | collective-permute-start | bytes 1376264 | tf_op jit(solution)/shard_map/ppermute | solution.py:45
  56.6 0.8 copy-start.7
  57.4 10.6 %collective-permute-start.5 = (bf16[448,512]{1,0:T(8,128)(2,1)S(1)}, bf16[448,512]{1,0:T(8,128)(2,1)S(1)}, u32[]{:S(2)}, u32[]{:S(2)}) collective-permute-start(bf16[448,512]{1,0:T(8,128)(2,1)S(1)} %collective-permute-done.4), channel_id=1, source_target_pairs={{0,1},{1,2},{2,3},{3,4},{4,5},{5,6},{6,7},{7,8},{8,9},{9,10},{10,1... | collective-permute-start | bytes 1376264 | tf_op jit(solution)/shard_map/ppermute | solution.py:45
  68.0 0.8 copy-start.9
  68.8 10.6 %collective-permute-start.6 = (bf16[448,512]{1,0:T(8,128)(2,1)S(1)}, bf16[448,512]{1,0:T(8,128)(2,1)S(1)}, u32[]{:S(2)}, u32[]{:S(2)}) collective-permute-start(bf16[448,512]{1,0:T(8,128)(2,1)S(1)} %collective-permute-done.5), channel_id=1, source_target_pairs={{0,1},{1,2},{2,3},{3,4},{4,5},{5,6},{6,7},{7,8},{8,9},{9,10},{10,1... | collective-permute-start | bytes 1376264 | tf_op jit(solution)/shard_map/ppermute | solution.py:45
  79.4 10.8 %copy-start.11 = (bf16[448,512]{1,0:T(8,128)(2,1)}, bf16[448,512]{1,0:T(8,128)(2,1)S(1)}, u32[]{:S(2)}) copy-start(bf16[448,512]{1,0:T(8,128)(2,1)S(1)} %collective-permute-done.6) | copy-start | bytes 1376260
  79.4 10.6 %collective-permute-start.7 = (bf16[448,512]{1,0:T(8,128)(2,1)S(1)}, bf16[448,512]{1,0:T(8,128)(2,1)S(1)}, u32[]{:S(2)}, u32[]{:S(2)}) collective-permute-start(bf16[448,512]{1,0:T(8,128)(2,1)S(1)} %collective-permute-done.6), channel_id=1, source_target_pairs={{0,1},{1,2},{2,3},{3,4},{4,5},{5,6},{6,7},{7,8},{8,9},{9,10},{10,1... | collective-permute-start | bytes 1376264 | tf_op jit(solution)/shard_map/ppermute | solution.py:45
  90.0 12.5 %copy-start.13 = (bf16[448,512]{1,0:T(8,128)(2,1)}, bf16[448,512]{1,0:T(8,128)(2,1)S(1)}, u32[]{:S(2)}) copy-start(bf16[448,512]{1,0:T(8,128)(2,1)S(1)} %collective-permute-done.7) | copy-start | bytes 1376260
  90.0 10.6 %collective-permute-start.8 = (bf16[448,512]{1,0:T(8,128)(2,1)S(1)}, bf16[448,512]{1,0:T(8,128)(2,1)S(1)}, u32[]{:S(2)}, u32[]{:S(2)}) collective-permute-start(bf16[448,512]{1,0:T(8,128)(2,1)S(1)} %collective-permute-done.7), channel_id=1, source_target_pairs={{0,1},{1,2},{2,3},{3,4},{4,5},{5,6},{6,7},{7,8},{8,9},{9,10},{10,1... | collective-permute-start | bytes 1376264 | tf_op jit(solution)/shard_map/ppermute | solution.py:45
  100.6 55.4 %copy-start.15 = (bf16[448,512]{1,0:T(8,128)(2,1)}, bf16[448,512]{1,0:T(8,128)(2,1)S(1)}, u32[]{:S(2)}) copy-start(bf16[448,512]{1,0:T(8,128)(2,1)S(1)} %collective-permute-done.8) | copy-start | bytes 1376260
  100.6 10.6 %collective-permute-start.9 = (bf16[448,512]{1,0:T(8,128)(2,1)S(1)}, bf16[448,512]{1,0:T(8,128)(2,1)S(1)}, u32[]{:S(2)}, u32[]{:S(2)}) collective-permute-start(bf16[448,512]{1,0:T(8,128)(2,1)S(1)} %collective-permute-done.8), channel_id=1, source_target_pairs={{0,1},{1,2},{2,3},{3,4},{4,5},{5,6},{6,7},{7,8},{8,9},{9,10},{10,1... | collective-permute-start | bytes 1376264 | tf_op jit(solution)/shard_map/ppermute | solution.py:45
  102.5 53.5 %all-to-all-start = ((bf16[16,4,7168]{2,1,0:T(4,128)(2,1)}), bf16[16,4,7168]{2,1,0:T(4,128)(2,1)S(1)}, u32[]{:S(2)}, u32[]{:S(2)}) async-start(bf16[16,4,7168]{2,1,0:T(4,128)(2,1)} %bitcast.2), calls=%async_computation | async-start | bytes 1835008 | tf_op jit(solution)/shard_map/all_to_all | solution.py:52
  111.2 44.8 %copy-start.17 = (bf16[448,512]{1,0:T(8,128)(2,1)}, bf16[448,512]{1,0:T(8,128)(2,1)S(1)}, u32[]{:S(2)}) copy-start(bf16[448,512]{1,0:T(8,128)(2,1)S(1)} %collective-permute-done.9) | copy-start | bytes 1376260
  111.2 22.8 %collective-permute-start.10 = (bf16[448,512]{1,0:T(8,128)(2,1)S(1)}, bf16[448,512]{1,0:T(8,128)(2,1)S(1)}, u32[]{:S(2)}, u32[]{:S(2)}) collective-permute-start(bf16[448,512]{1,0:T(8,128)(2,1)S(1)} %collective-permute-done.9), channel_id=1, source_target_pairs={{0,1},{1,2},{2,3},{3,4},{4,5},{5,6},{6,7},{7,8},{8,9},{9,10},{10,1... | collective-permute-start | bytes 1376264 | tf_op jit(solution)/shard_map/ppermute | solution.py:45
  134.0 32.2 %copy-start.19 = (bf16[448,512]{1,0:T(8,128)(2,1)}, bf16[448,512]{1,0:T(8,128)(2,1)S(1)}, u32[]{:S(2)}) copy-start(bf16[448,512]{1,0:T(8,128)(2,1)S(1)} %collective-permute-done.10) | copy-start | bytes 1376260
  134.0 10.6 %collective-permute-start.11 = (bf16[448,512]{1,0:T(8,128)(2,1)S(1)}, bf16[448,512]{1,0:T(8,128)(2,1)S(1)}, u32[]{:S(2)}, u32[]{:S(2)}) collective-permute-start(bf16[448,512]{1,0:T(8,128)(2,1)S(1)} %collective-permute-done.10), channel_id=1, source_target_pairs={{0,1},{1,2},{2,3},{3,4},{4,5},{5,6},{6,7},{7,8},{8,9},{9,10},{10,1... | collective-permute-start | bytes 1376264 | tf_op jit(solution)/shard_map/ppermute | solution.py:45
  144.6 21.6 %copy-start.21 = (bf16[448,512]{1,0:T(8,128)(2,1)}, bf16[448,512]{1,0:T(8,128)(2,1)S(1)}, u32[]{:S(2)}) copy-start(bf16[448,512]{1,0:T(8,128)(2,1)S(1)} %collective-permute-done.11) | copy-start | bytes 1376260
  144.6 10.7 %collective-permute-start.12 = (bf16[448,512]{1,0:T(8,128)(2,1)S(1)}, bf16[448,512]{1,0:T(8,128)(2,1)}, u32[]{:S(2)}, u32[]{:S(2)}) collective-permute-start(bf16[448,512]{1,0:T(8,128)(2,1)S(1)} %collective-permute-done.11), channel_id=1, source_target_pairs={{0,1},{1,2},{2,3},{3,4},{4,5},{5,6},{6,7},{7,8},{8,9},{9,10},{10,1... | collective-permute-start | bytes 1376264 | tf_op jit(solution)/shard_map/ppermute | solution.py:45
  155.3 10.9 %collective-permute-start.13 = (bf16[448,512]{1,0:T(8,128)(2,1)}, bf16[448,512]{1,0:T(8,128)(2,1)}, u32[]{:S(2)}, u32[]{:S(2)}) collective-permute-start(bf16[448,512]{1,0:T(8,128)(2,1)} %collective-permute-done.12), channel_id=1, source_target_pairs={{0,1},{1,2},{2,3},{3,4},{4,5},{5,6},{6,7},{7,8},{8,9},{9,10},{10,1... | collective-permute-start | bytes 1376264 | tf_op jit(solution)/shard_map/ppermute | solution.py:45
  156.2 35.7 %copy-start = (bf16[448,512]{1,0:T(8,128)(2,1)S(1)}, bf16[448,512]{1,0:T(8,128)(2,1)}, u32[]{:S(2)}) copy-start(bf16[448,512]{1,0:T(8,128)(2,1)} %param.13) | copy-start | bytes 1376260
  166.2 10.9 %collective-permute-start.14 = (bf16[448,512]{1,0:T(8,128)(2,1)}, bf16[448,512]{1,0:T(8,128)(2,1)}, u32[]{:S(2)}, u32[]{:S(2)}) collective-permute-start(bf16[448,512]{1,0:T(8,128)(2,1)} %collective-permute-done.13), channel_id=1, source_target_pairs={{0,1},{1,2},{2,3},{3,4},{4,5},{5,6},{6,7},{7,8},{8,9},{9,10},{10,1... | collective-permute-start | bytes 1376264 | tf_op jit(solution)/shard_map/ppermute | solution.py:45
  171.7 24.0 %copy-start.2 = (bf16[448,512]{1,0:T(8,128)(2,1)S(1)}, bf16[448,512]{1,0:T(8,128)(2,1)}, u32[]{:S(2)}) copy-start(bf16[448,512]{1,0:T(8,128)(2,1)} %copy-done.1) | copy-start | bytes 1376260
  172.0 23.1 %copy-start.22 = (bf16[448,512]{1,0:T(8,128)(2,1)S(1)}, bf16[448,512]{1,0:T(8,128)(2,1)}, u32[]{:S(2)}) copy-start(bf16[448,512]{1,0:T(8,128)(2,1)} %copy-done.21) | copy-start | bytes 1376260
  172.0 23.2 %copy-start.20 = (bf16[448,512]{1,0:T(8,128)(2,1)S(1)}, bf16[448,512]{1,0:T(8,128)(2,1)}, u32[]{:S(2)}) copy-start(bf16[448,512]{1,0:T(8,128)(2,1)} %copy-done.19) | copy-start | bytes 1376260
  172.1 23.2 %copy-start.18 = (bf16[448,512]{1,0:T(8,128)(2,1)S(1)}, bf16[448,512]{1,0:T(8,128)(2,1)}, u32[]{:S(2)}) copy-start(bf16[448,512]{1,0:T(8,128)(2,1)} %copy-done.17) | copy-start | bytes 1376260
  172.1 23.2 %copy-start.16 = (bf16[448,512]{1,0:T(8,128)(2,1)S(1)}, bf16[448,512]{1,0:T(8,128)(2,1)}, u32[]{:S(2)}) copy-start(bf16[448,512]{1,0:T(8,128)(2,1)} %copy-done.15) | copy-start | bytes 1376260
  172.1 23.3 %copy-start.14 = (bf16[448,512]{1,0:T(8,128)(2,1)S(1)}, bf16[448,512]{1,0:T(8,128)(2,1)}, u32[]{:S(2)}) copy-start(bf16[448,512]{1,0:T(8,128)(2,1)} %copy-done.13) | copy-start | bytes 1376260
  172.1 23.3 %copy-start.12 = (bf16[448,512]{1,0:T(8,128)(2,1)S(1)}, bf16[448,512]{1,0:T(8,128)(2,1)}, u32[]{:S(2)}) copy-start(bf16[448,512]{1,0:T(8,128)(2,1)} %copy-done.11) | copy-start | bytes 1376260
  172.1 23.4 %copy-start.10 = (bf16[448,512]{1,0:T(8,128)(2,1)S(1)}, bf16[448,512]{1,0:T(8,128)(2,1)}, u32[]{:S(2)}) copy-start(bf16[448,512]{1,0:T(8,128)(2,1)} %copy-done.9) | copy-start | bytes 1376260
  172.1 23.4 %copy-start.8 = (bf16[448,512]{1,0:T(8,128)(2,1)S(1)}, bf16[448,512]{1,0:T(8,128)(2,1)}, u32[]{:S(2)}) copy-start(bf16[448,512]{1,0:T(8,128)(2,1)} %copy-done.7) | copy-start | bytes 1376260
  172.1 23.4 %copy-start.6 = (bf16[448,512]{1,0:T(8,128)(2,1)S(1)}, bf16[448,512]{1,0:T(8,128)(2,1)}, u32[]{:S(2)}) copy-start(bf16[448,512]{1,0:T(8,128)(2,1)} %copy-done.5) | copy-start | bytes 1376260
  172.1 23.5 %copy-start.4 = (bf16[448,512]{1,0:T(8,128)(2,1)S(1)}, bf16[448,512]{1,0:T(8,128)(2,1)}, u32[]{:S(2)}) copy-start(bf16[448,512]{1,0:T(8,128)(2,1)} %copy-done.3) | copy-start | bytes 1376260
  187.7 14.4 %copy-start.23 = (s32[4,2]{0,1:T(2,128)S(1)}, s32[4,2]{0,1:T(2,128)}, u32[]{:S(2)}) copy-start(s32[4,2]{0,1:T(2,128)} %param.9) | copy-start | bytes 100
  198.6 11.4 %all-to-all-start.1 = ((f32[16,4,512]{2,1,0:T(4,128)}), f32[16,4,512]{2,1,0:T(4,128)S(1)}, u32[]{:S(2)}, u32[]{:S(2)}) async-start(f32[16,4,512]{2,1,0:T(4,128)} %copy.27), calls=%async_computation.1 | async-start | bytes 262144 | tf_op jit(solution)/shard_map/all_to_all | solution.py:58
